TPU v7x, 32 devices: a whole 2x2x4 slice. The times are simulated.
32 devices in a mesh: group: 2 (over y), swap: 8 (over z, x), image: 2 (over core).
Axes of the slice: x: 2, y: 2, z: 4, core: 2. Of those that a mesh axis runs over, the one named last changes fastest.
Arguments:
- images_in: bfloat16 [16, 1536, 4096], P(('group', 'image'), 'swap'), parts along dimension 0, may hold values from -6 to 6
- kernel: bfloat16 [1536, 49], P('swap'), may hold values from -1.75 to 1.75
- conv_bias: float32 [1536], P('swap'), may hold values from -1 to 1
- norm_gain: float32 [1536], replicated, may hold values from 0.1 to 1.9
- norm_shift: float32 [1536], replicated, may hold values from -0.5 to 0.5
- fp8_weight: bfloat16 [1536, 6144], P('swap', 'image'), may hold values from -1.875 to 1.875, as said below
- block_scale: int32 [1536, 48], P('swap', 'image'), may hold values from -7 to -5
- adapter_a: bfloat16 [1536, 32], replicated, may hold values from -0.15625 to 0.15625
- adapter_b: bfloat16 [32, 6144], P(None, 'image'), may hold values from -0.25 to 0.25
- cotangent: bfloat16 [16, 4096, 6144], P('group', 'swap', 'image'), parts along dimension 0, may hold values from -0.05 to 0.05
Outputs:
- grad_a: float32 [3072, 32], P('group'), parts along dimension 0
- grad_b: float32 [64, 6144], P('group', 'image'), parts along dimension 0
There are 2 independent parts, one for each index of `group`. A program takes and returns all parts, laid end to end along the dimension named above; an argument that names none is the same for every part. Nothing has to cross between parts.
Inputs may be any that keep to these rules, and one draw needn't show every extreme that they name: `fp8_weight`: each entry is a value of the E4M3 format: a sign times 2 to an integer power times 1 + k / 8 for an integer k of 0 to 7. `block_scale`: the entry at [c, j] is the exponent of the scale of hidden units 128 * j to 128 * j + 127 of weight row c.
All inputs are finite; a program needn't handle non-finite values.
Results may differ from a plain program's by a relative error of at most 0.00055.
The roundings to bfloat16 on the way count: a program that leaves them out, or rounds other values in their place, can miss the bound.
Values may be sent and summed in bfloat16 or wider, within the bound.
A program may use at most 192 MiB of HBM per device.

v0:
```python
import jax
import jax.numpy as jnp
from jax import lax
from jax.sharding import PartitionSpec as P

KS = 7
W = 64
adapter_scale = 2.0
norm_eps = 1e-06


def power_table(scales):
    factor = jnp.zeros(scales.shape, jnp.float32)
    for exponent in range(-12, 4):
        factor = factor + jnp.where(
            scales == exponent, jnp.float32(2.0**exponent), jnp.float32(0.0)
        )
    return factor


def decode(weight, scales):
    row_count = weight.shape[0]
    groups = scales.shape[1]
    blocks = (
        weight.reshape(row_count, groups, -1).astype(jnp.float32) * power_table(scales)[:, :, None]
    )
    return blocks.reshape(row_count, -1).astype(jnp.bfloat16)


def gelu_slope(pre_act):
    cumulative = 0.5 * (1.0 + jax.scipy.special.erf(pre_act * 0.7071067811865476))
    density = jnp.exp(-0.5 * pre_act * pre_act) * 0.3989422804014327
    return cumulative + pre_act * density


def depthwise(images, kernel, conv_bias, map_width):
    batch, channels, pixels = images.shape
    maps = images.reshape(batch, channels, pixels // map_width, map_width)
    taps = kernel.reshape(channels, 1, KS, KS)
    half_span = KS // 2
    summed = lax.conv_general_dilated(
        maps,
        taps,
        (1, 1),
        ((half_span, half_span), (half_span, half_span)),
        dimension_numbers=("NCHW", "OIHW", "NCHW"),
        feature_group_count=channels,
        preferred_element_type=jnp.float32,
    )
    summed = summed.reshape(batch, channels, pixels)
    return summed + conv_bias[None, :, None]


def shards(
    images_in,
    kernel,
    conv_bias,
    norm_gain,
    norm_shift,
    fp8_weight,
    block_scale,
    adapter_a,
    adapter_b,
    cotangent,
):
    conv = depthwise(images_in, kernel, conv_bias, W).astype(jnp.bfloat16)
    values = lax.all_to_all(conv, "swap", split_axis=2, concat_axis=1, tiled=True).astype(
        jnp.float32
    )
    average = jnp.mean(values, axis=1, keepdims=True)
    centred = values - average
    variance = jnp.mean(centred * centred, axis=1, keepdims=True)
    scaled = (
        centred * lax.rsqrt(variance + norm_eps) * norm_gain[None, :, None]
        + norm_shift[None, :, None]
    )
    normed = jnp.swapaxes(scaled, 1, 2).astype(jnp.bfloat16)
    own_rows = normed.reshape(-1, normed.shape[2])
    tokens = lax.all_gather(own_rows, "image", axis=0, tiled=True)
    zero_start = jnp.zeros((tokens.shape[0], fp8_weight.shape[1]), jnp.float32)
    local_weight = decode(fp8_weight, block_scale)
    shard_rows = lax.all_gather(local_weight, "swap", axis=0, tiled=True)
    columns = lax.slice_in_dim(tokens, 0, shard_rows.shape[0], axis=1)
    frozen = zero_start + jnp.dot(columns, shard_rows, preferred_element_type=jnp.float32)
    low_rank = jnp.dot(tokens, adapter_a, preferred_element_type=jnp.float32).astype(jnp.bfloat16)
    pre_act = frozen + adapter_scale * jnp.dot(
        low_rank, adapter_b, preferred_element_type=jnp.float32
    )
    upstream = cotangent.reshape(-1, cotangent.shape[2])
    grad_pre = (upstream.astype(jnp.float32) * gelu_slope(pre_act)).astype(jnp.bfloat16)
    grad_b_local = adapter_scale * jnp.dot(low_rank.T, grad_pre, preferred_element_type=jnp.float32)
    partial_back = jnp.dot(grad_pre, adapter_b.T, preferred_element_type=jnp.float32)
    contract = (((0,), (0,)), ((), ()))
    tokens_wide = tokens.astype(jnp.float32)
    summed_back = lax.psum(partial_back, "image")
    grad_a_local = adapter_scale * lax.dot_general(
        tokens_wide,
        summed_back,
        contract,
        precision=lax.Precision.HIGHEST,
        preferred_element_type=jnp.float32,
    )
    grad_a, grad_b = lax.psum((grad_a_local, grad_b_local), "swap")
    return (grad_a, grad_b)


def solution(mesh):
    placed = (
        P(("group", "image"), "swap", None),
        P("swap", None),
        P("swap"),
        P(),
        P(),
        P("swap", "image"),
        P("swap", "image"),
        P(),
        P(None, "image"),
        P("group", "swap", "image"),
    )
    return jax.shard_map(
        shards,
        mesh=mesh,
        in_specs=placed,
        out_specs=(P("group", None), P("group", "image")),
        check_vma=False,
    )
```

profile of v0, /device:TPU:0, one launch (start us, length us, event | category | flops | bytes accessed | tf_op | source)
XLA Modules:
  0.0 837.5 jit_solution(14557225846373415734)
XLA Ops:
  7.2 0.0 copy-start
  7.2 0.0 all-gather.3.cloned.1.call-start
  7.2 0.8 reshape.62
  8.1 10.6 %copy.43 = bf16[4,192,4096]{1,2,0:T(8,128)(2,1)} copy(bf16[4,192,4096]{2,1,0:T(8,128)(2,1)} %param.10) | data formatting | bytes 12582912 | tf_op args[0]
  18.7 11.5 %copy.54 = bf16[192,64,4,64]{0,1,3,2:T(8,128)(2,1)} copy(bf16[192,64,4,64]{0,3,1,2:T(8,128)(2,1)} %bitcast.75) | data formatting | bytes 12582912
  30.2 10.0 %pad.clone = bf16[192,64,4,72]{0,1,3,2:T(8,128)(2,1)} pad(bf16[192,64,4,64]{0,1,3,2:T(8,128)(2,1)} %copy.54, bf16[]{:T(256)} %constant.37), padding=0_0x0_0x0_0x3_5 | pad | bytes 13369346 | tf_op jit(solution)/shard_map/reshape | solution.py:38
  40.2 3.4 slice.2
  43.7 1.9 copy-done.2
  45.5 4.2 fusion.8
  49.7 95.5 %broadcast_select_fusion = f32[64,32,9,192]{3,1,2,0:T(8,128)S(1)} fusion(pred[32,9]{0,1:T(8,128)(4,1)S(1)} %copy-done.9, bf16[192,1,7,7]{0,1,3,2:T(2,128)(2,1)S(1)} %reshape.62, bf16[192,64,4,8,15]{0,1,4,3,2:T(8,128)(2,1)S(1)} %fusion.8), kind=kOutput, calls=%fused_computation.23 | convolution fusion | flops 341065728 | bytes 25971360 | tf_op jit(solution)/shard_map/conv_general_dilated | solution.py:41
  145.3 20.1 %copy.47 = f32[64,32,9,192]{3,0,2,1:T(8,128)S(1)} copy(f32[64,32,9,192]{3,1,2,0:T(8,128)S(1)} %broadcast_select_fusion) | data formatting | bytes 28311552 | tf_op jit(solution)/shard_map/conv_general_dilated | solution.py:41
  165.4 2.0 slice_bitcast_fusion
  167.4 0.0 copy-start.8
  167.4 17.9 %copy.48 = f32[4,192,64,64]{1,3,2,0:T(8,128)S(1)} copy(f32[4,192,64,64]{1,2,3,0:T(8,128)S(1)} %slice_bitcast_fusion) | data formatting | bytes 25165824 | tf_op jit(solution)/shard_map/conv_general_dilated | solution.py:41
  185.3 2.5 fusion.7
  187.9 31.9 %copy.49 = bf16[4,192,4096]{1,0,2:T(4,128)(2,1)S(1)} copy(bf16[4,192,4096]{1,2,0:T(8,128)(2,1)S(1)} %fusion.7) | data formatting | bytes 12582912 | tf_op jit(solution)/shard_map/convert_element_type | solution.py:66
  219.8 190.2 %all_to_all.4 = bf16[4,192,4096]{1,0,2:T(4,128)(2,1)} all-to-all(bf16[4,192,4096]{1,0,2:T(4,128)(2,1)S(1)} %copy.49), channel_id=1, replica_groups=mesh['group'=2,'swap'=8,'image'=2] {'swap'}, dimensions={2} | all-to-all | bytes 12582912 | tf_op jit(solution)/shard_map/all_to_all | solution.py:67
  410.0 13.5 %copy.50 = bf16[4,192,4096]{2,1,0:T(8,128)(2,1)} copy(bf16[4,192,4096]{1,0,2:T(4,128)(2,1)} %all_to_all.4) | data formatting | bytes 12582912 | tf_op jit(solution)/shard_map/all_to_all | solution.py:67
  423.6 9.1 %copy.55 = f32[96,8,8,512]{3,2,1,0:T(8,128)S(1)} copy(bf16[96,8,8,512]{3,1,2,0:T(8,128)(2,1)} %bitcast.77) | data formatting | bytes 18874368
  432.6 1.0 fusion.19
  433.6 3.5 copy-done.1
  437.1 1.6 multiply_reduce_fusion
  438.7 10.6 %bitcast_bitcast_fusion = f32[4,8,192,512]{3,1,2,0:T(8,128)} fusion(f32[4,192,8,512]{3,2,1,0:T(8,128)} %bitcast.71), kind=kLoop, calls=%fused_computation.16 | loop fusion | bytes 25165824 | tf_op jit(solution)/shard_map/convert_element_type | solution.py:67
  449.4 16.7 %copy.51 = f32[4,8,192,512]{3,2,1,0:T(8,128)} copy(f32[4,8,192,512]{3,1,2,0:T(8,128)} %bitcast_bitcast_fusion) | data formatting | bytes 25165824 | tf_op jit(solution)/shard_map/convert_element_type | solution.py:67
  466.1 9.0 %fusion.15 = bf16[4,1536,512]{2,1,0:T(8,128)(2,1)} fusion(f32[4,8,192,512]{3,2,1,0:T(8,128)} %copy.51, f32[1536]{0:T(1024)S(1)} %copy-done.6, f32[1536]{0:T(1024)S(1)} %copy-done.7, f32[4,512]{1,0:T(4,128)S(1)} %add_rsqrt_fusion, f32[4,512]{1,0:T(4,128)S(1)} %broadcast_multiply_fusion), kind=kLoop, calls=%fused_computation.21 | loop fusion | flops 15728640 | bytes 18903040 | tf_op jit(solution)/shard_map/convert_element_type | solution.py:77
  475.1 8.7 %copy.52 = bf16[4,512,1536]{2,1,0:T(8,128)(2,1)} copy(bf16[4,512,1536]{1,2,0:T(8,128)(2,1)} %bitcast.78) | data formatting | bytes 12582912 | tf_op jit(solution)/shard_map/convert_element_type | solution.py:77
  483.8 0.0 all-gather.3.cloned.1.call-update
  483.8 0.0 all-gather.5.cloned.1.call-start
  483.9 0.1 copy.53
  484.0 0.7 mul.87
  484.7 1.6 fusion.18
  486.4 0.0 all-gather.5.cloned.1.call-update
  486.4 0.0 all-reduce.4.cloned.1.call-start
  486.4 21.3 %all-gather.3.cloned.1.call-done = bf16[4096,1536]{1,0:T(8,128)(2,1)} async-done(((bf16[2048,1536]{1,0:T(8,128)(2,1)}), bf16[4096,1536]{1,0:T(8,128)(2,1)}) %all-gather.3.cloned.1.call-update) | async-done | bytes 12582928 | tf_op jit(solution)/shard_map/all_gather | solution.py:79
  507.7 8.3 convolution_convert_fusion
  516.0 20.1 %fusion.20 = f32[4096,3072]{1,0:T(8,128)} fusion(bf16[4096,32]{0,1:T(8,128)(2,1)S(1)} %convolution_convert_fusion, bf16[32,3072]{1,0:T(8,128)(2,1)S(1)} %copy-done), kind=kOutput, calls=%fused_computation.33 | convolution fusion | flops 805306368 | bytes 50790400 | tf_op jit(solution)/shard_map/dot_general | solution.py:86
  536.2 112.2 %all-gather.5.cloned.1.call-done = bf16[1536,3072]{1,0:T(8,128)(2,1)} async-done(((bf16[192,3072]{1,0:T(8,128)(2,1)}), bf16[1536,3072]{1,0:T(8,128)(2,1)}) %all-gather.5.cloned.1.call-update) | async-done | bytes 9437200 | tf_op jit(solution)/shard_map/all_gather | solution.py:82
  648.3 64.7 %fusion.5 = bf16[4096,3072]{1,0:T(8,128)(2,1)} fusion(bf16[4096,3072]{1,0:T(8,128)(2,1)} %bitcast.80, f32[4096,3072]{1,0:T(8,128)} %fusion.20, bf16[4096,1536]{1,0:T(8,128)(2,1)} %all-gather.3.cloned.1.call-done, bf16[1536,3072]{1,0:T(8,128)(2,1)} %all-gather.5.cloned.1.call-done), kind=kOutput, calls=%fused_computation.6 | convolution fusion | flops 38818283520 | bytes 122683392 | tf_op jit(solution)/shard_map/dot_general | solution.py:84
  713.0 12.9 %fusion.21 = f32[4096,32]{0,1:T(8,128)} fusion(bf16[4096,3072]{1,0:T(8,128)(2,1)} %fusion.5, bf16[32,3072]{1,0:T(8,128)(2,1)S(1)} %copy-done), kind=kOutput, calls=%fused_computation.34 | convolution fusion | flops 805306368 | bytes 25886720 | tf_op jit(solution)/shard_map/dot_general | solution.py:92
  725.9 0.0 all-reduce.4.cloned.1.call-update
  725.9 0.0 all-reduce.6.cloned.1.call-start
  726.0 11.7 %convolution_multiply_fusion = f32[32,3072]{1,0:T(8,128)} fusion(bf16[4096,32]{0,1:T(8,128)(2,1)S(1)} %convolution_convert_fusion, bf16[4096,3072]{1,0:T(8,128)(2,1)} %fusion.5), kind=kOutput, calls=%fused_computation.25 | convolution fusion | flops 805404672 | bytes 25821184 | tf_op jit(solution)/shard_map/dot_general | solution.py:91
  737.7 5.2 all-reduce.4.cloned.1.call-done
  742.8 9.8 %convolution_multiply_fusion.1 = f32[1536,32]{0,1:T(8,128)} fusion(bf16[4096,1536]{1,0:T(8,128)(2,1)} %all-gather.3.cloned.1.call-done, f32[4096,32]{0,1:T(8,128)} %all-reduce.4.cloned.1.call-done), kind=kOutput, calls=%fused_computation.28 | convolution fusion | flops 2415968256 | bytes 13303808 | tf_op jit(solution)/shard_map/dot_general | solution.py:96
  752.6 0.0 all-reduce.6.cloned.1.call-update
  752.7 74.7 %all-reduce.6.cloned.1.call-done = (f32[1536,32]{0,1:T(8,128)}, f32[32,3072]{1,0:T(8,128)}) async-done(((f32[1536,32]{0,1:T(8,128)}, f32[32,3072]{1,0:T(8,128)}), (f32[1536,32]{0,1:T(8,128)}, f32[32,3072]{1,0:T(8,128)})) %all-reduce.6.cloned.1.call-update) | async-done | bytes 589840 | tf_op jit(solution)/shard_map/psum | solution.py:103
  827.3 1.6 copy.67
  829.0 1.8 copy.68
  (19 shorter events, 0.1 us)
Async XLA Ops:
  7.2 508.9 %copy-start = (bf16[32,3072]{1,0:T(8,128)(2,1)S(1)}, bf16[32,3072]{1,0:T(8,128)(2,1)}, u32[]{:S(2)}) copy-start(bf16[32,3072]{1,0:T(8,128)(2,1)} %param.18) | copy-start | bytes 589828
  7.2 500.5 %all-gather.3.cloned.1.call-start = ((), (), s32[]{:S(2)}) async-start(), calls=%async_computation.1 | async-start | bytes 18874368 | tf_op jit(solution)/shard_map/all_gather | solution.py:79
  40.2 5.3 copy-start.2
  45.5 4.2 copy-start.9
  167.4 17.9 %copy-start.8 = (f32[192]{0:T(256)S(1)}, f32[192]{0:T(256)}, u32[]{:S(2)}) copy-start(f32[192]{0:T(256)} %param.12) | copy-start | bytes 2308
  432.6 4.5 copy-start.1
  449.4 16.8 %copy-start.6 = (f32[1536]{0:T(1024)S(1)}, f32[1536]{0:T(1024)}, u32[]{:S(2)}) copy-start(f32[1536]{0:T(1024)} %param.14) | copy-start | bytes 18436
  449.4 16.8 %copy-start.7 = (f32[1536]{0:T(1024)S(1)}, f32[1536]{0:T(1024)}, u32[]{:S(2)}) copy-start(f32[1536]{0:T(1024)} %param.13) | copy-start | bytes 18436
  466.1 17.8 %copy-start.5 = (s32[192,24]{0,1:T(8,128)S(1)}, s32[192,24]{0,1:T(8,128)}, u32[]{:S(2)}) copy-start(s32[192,24]{0,1:T(8,128)} %param.16) | copy-start | bytes 55300
  466.1 18.6 %copy-start.3 = (bf16[192,3072]{1,0:T(8,128)(2,1)S(1)}, bf16[192,3072]{1,0:T(8,128)(2,1)}, u32[]{:S(2)}) copy-start(bf16[192,3072]{1,0:T(8,128)(2,1)} %param.15) | copy-start | bytes 3538948
  475.1 32.6 %copy-start.4 = (bf16[1536,32]{0,1:T(8,128)(2,1)S(1)}, bf16[1536,32]{0,1:T(8,128)(2,1)}, u32[]{:S(2)}) copy-start(bf16[1536,32]{0,1:T(8,128)(2,1)} %param.17) | copy-start | bytes 294916
  483.8 164.5 %all-gather.5.cloned.1.call-start = ((), (), s32[]{:S(2)}) async-start(), calls=%async_computation.2 | async-start | bytes 10616832 | tf_op jit(solution)/shard_map/all_gather | solution.py:82
  486.4 256.5 %all-reduce.4.cloned.1.call-start = ((), (), s32[]{:S(2)}) async-start(), calls=%async_computation.3 | async-start | bytes 1048576 | tf_op jit(solution)/shard_map/psum | solution.py:95
  725.9 101.4 %all-reduce.6.cloned.1.call-start = ((), (), s32[]{:S(2)}) async-start(), calls=%async_computation.4 | async-start | bytes 1179648 | tf_op jit(solution)/shard_map/psum | solution.py:103
Sparse Core Ops, SparseCore 0:
  484.0 23.7 all-gather.2
  509.9 138.3 all-gather.4
  726.0 16.7 all-reduce.3
  752.8 74.5 all-reduce.5
where the time goes:
time: 845 us; the launch traced here: 837 us
  matrix products  223 us (26%)
  waiting for transfers between devices  213 us (25%)
  blocking collectives  190 us (22%)
  local copies, waits for them, and re-layouts  176 us (21%)
  other arithmetic  20 us (2%)
  between operations  14.2 us (2%)
    all_to_all x1, blocking collectives, shards(): lax.all_to_all(conv, 'swap', split_axis=2, concat_axis=1, tiled=True)  190 us
    all_gather x1, waiting for transfers between devices, shards(): shard_rows = lax.all_gather(local_weight, 'swap', axis=0, tiled=True)  112 us
    conv_general_dilated x1, matrix products, depthwise(): lax.conv_general_dilated(maps, taps, (1, 1), ((half_span, half_span), (ha...  95.5 us
    psum x1, waiting for transfers between devices, shards(): grad_a, grad_b = lax.psum((grad_a_local, grad_b_local), 'swap')  74.7 us
    dot_general x1, matrix products, shards(): jnp.dot(columns, shard_rows, preferred_element_type=jnp.float32)  64.7 us
    conv_general_dilated x4, local copies, waits for them, and re-layouts, depthwise(): lax.conv_general_dilated(maps, taps, (1, 1), ((half_span, half_span), (ha...  43.4 us
    unnamed x25, local copies, waits for them, and re-layouts  40 us
    convert_element_type x1, local copies, waits for them, and re-layouts, shards(): conv = depthwise(images_in, kernel, conv_bias, W).astype(jnp.bfloat16)  31.9 us
  transfers between devices with their start and end apart: 4, of which 4 were waited for; matrix products, arithmetic and copies ran while one was open for 5% of the time, Pallas kernels for 0%

commit v1 on v0

--- a/solution.py
+++ b/solution.py
@@ -7,6 +7,12 @@
 W = 64
 adapter_scale = 2.0
 norm_eps = 1e-06
+
+
+def swap_blocks(block, mesh_axis, split, join):
+    cells = jnp.split(block, lax.axis_size(mesh_axis), axis=split)
+    received = lax.all_to_all(jnp.stack(cells), mesh_axis, 0, 0)
+    return jnp.concatenate(received, axis=join)
 
 
 def power_table(scales):
@@ -64,9 +70,7 @@
     cotangent,
 ):
     conv = depthwise(images_in, kernel, conv_bias, W).astype(jnp.bfloat16)
-    values = lax.all_to_all(conv, "swap", split_axis=2, concat_axis=1, tiled=True).astype(
-        jnp.float32
-    )
+    values = swap_blocks(conv, "swap", 2, 1).astype(jnp.float32)
     average = jnp.mean(values, axis=1, keepdims=True)
     centred = values - average
     variance = jnp.mean(centred * centred, axis=1, keepdims=True)

time: 845 us -> 731 us (0.87)
  local copies, waits for them, and re-layouts: 176 us -> 111 us
  blocking collectives: 190 us -> 146 us
    convert_element_type x3 -> x0, local copies, waits for them, and re-layouts: 59.2 us -> none  [the longest x1 31.9 us: shards(): conv = depthwise(images_in, kernel, conv_bias, W).astype(jnp.bfloat16)]
    all_to_all x1, blocking collectives: 190 us -> 146 us  [swap_blocks(): received = lax.all_to_all(jnp.stack(cells), mesh_axis, 0, 0)]
    all_to_all x1 -> x0, local copies, waits for them, and re-layouts: 13.5 us -> none  [shards(): lax.all_to_all(conv, 'swap', split_axis=2, concat_axis=1, tiled=True)]
    another operation x0 -> x2, local copies, waits for them, and re-layouts: none -> 12.2 us  [swap_blocks(): received = lax.all_to_all(jnp.stack(cells), mesh_axis, 0, 0)]
    unnamed x25 -> x29, local copies, waits for them, and re-layouts: 40 us -> 34.9 us
  transfers between devices with their start and end apart: 4 -> 4, of which waited for: 4 -> 4; matrix products, arithmetic and copies ran while one was open for 5% -> 6% of each run, Pallas kernels for 0% -> 0%
where the time goes in v1:
time: 731 us; the launch traced here: 723 us
  matrix products  223 us (31%)
  waiting for transfers between devices  213 us (29%)
  blocking collectives  146 us (20%)
  local copies, waits for them, and re-layouts  111 us (15%)
  other arithmetic  15.4 us (2%)
  between operations  14.2 us (2%)
    all_to_all x1, blocking collectives, swap_blocks(): received = lax.all_to_all(jnp.stack(cells), mesh_axis, 0, 0)  146 us
    all_gather x1, waiting for transfers between devices, shards(): shard_rows = lax.all_gather(local_weight, 'swap', axis=0, tiled=True)  112 us
    conv_general_dilated x1, matrix products, depthwise(): lax.conv_general_dilated(maps, taps, (1, 1), ((half_span, half_span), (ha...  95.7 us
    psum x1, waiting for transfers between devices, shards(): grad_a, grad_b = lax.psum((grad_a_local, grad_b_local), 'swap')  74.7 us
    dot_general x1, matrix products, shards(): jnp.dot(columns, shard_rows, preferred_element_type=jnp.float32)  64.7 us
    conv_general_dilated x4, local copies, waits for them, and re-layouts, depthwise(): lax.conv_general_dilated(maps, taps, (1, 1), ((half_span, half_span), (ha...  43.4 us
    unnamed x29, local copies, waits for them, and re-layouts  34.9 us
    all_gather x1, waiting for transfers between devices, shards(): tokens = lax.all_gather(own_rows, 'image', axis=0, tiled=True)  21.3 us
  transfers between devices with their start and end apart: 4, of which 4 were waited for; matrix products, arithmetic and copies ran while one was open for 6% of the time, Pallas kernels for 0%

profile of v1, /device:TPU:0, one launch (start us, length us, event | category | flops | bytes accessed | tf_op | source)
XLA Modules:
  0.0 723.2 jit_solution(9437239590115696736)
XLA Ops:
  7.2 0.0 all-gather.3.cloned.1.call-start
  7.2 0.8 reshape.58
  8.1 10.6 %copy.23 = bf16[4,192,4096]{1,2,0:T(8,128)(2,1)} copy(bf16[4,192,4096]{2,1,0:T(8,128)(2,1)} %param.10) | data formatting | bytes 12582912 | tf_op args[0]
  18.7 11.5 %copy.33 = bf16[192,64,4,64]{0,1,3,2:T(8,128)(2,1)} copy(bf16[192,64,4,64]{0,3,1,2:T(8,128)(2,1)} %bitcast.93) | data formatting | bytes 12582912
  30.2 10.0 %pad.clone = bf16[192,64,4,72]{0,1,3,2:T(8,128)(2,1)} pad(bf16[192,64,4,64]{0,1,3,2:T(8,128)(2,1)} %copy.33, bf16[]{:T(256)} %constant.37), padding=0_0x0_0x0_0x3_5 | pad | bytes 13369346 | tf_op jit(solution)/shard_map/reshape | solution.py:44
  40.2 3.4 slice.2
  43.6 1.9 copy-done.1
  45.5 4.2 fusion.8
  49.7 95.7 %broadcast_select_fusion = f32[64,32,9,192]{3,1,2,0:T(8,128)S(1)} fusion(pred[32,9]{0,1:T(8,128)(4,1)S(1)} %copy-done.8, bf16[192,1,7,7]{0,1,3,2:T(2,128)(2,1)S(1)} %reshape.58, bf16[192,64,4,8,15]{0,1,4,3,2:T(8,128)(2,1)S(1)} %fusion.8), kind=kOutput, calls=%fused_computation.25 | convolution fusion | flops 341065728 | bytes 25971360 | tf_op jit(solution)/shard_map/conv_general_dilated | solution.py:47
  145.4 20.1 %copy.27 = f32[64,32,9,192]{3,0,2,1:T(8,128)S(1)} copy(f32[64,32,9,192]{3,1,2,0:T(8,128)S(1)} %broadcast_select_fusion) | data formatting | bytes 28311552 | tf_op jit(solution)/shard_map/conv_general_dilated | solution.py:47
  165.5 2.0 slice_bitcast_fusion
  167.5 17.9 %copy.28 = f32[4,192,64,64]{1,3,2,0:T(8,128)S(1)} copy(f32[4,192,64,64]{1,2,3,0:T(8,128)S(1)} %slice_bitcast_fusion) | data formatting | bytes 25165824 | tf_op jit(solution)/shard_map/conv_general_dilated | solution.py:47
  185.4 2.5 fusion.7
  188.0 1.0 fusion.28
  189.0 1.1 fusion.27
  190.1 1.1 fusion.26
  191.2 1.1 fusion.25
  192.2 1.0 fusion.24
  193.3 1.1 fusion.23
  194.3 1.1 fusion.22
  195.4 1.1 fusion.21
  196.5 11.1 %copy.29 = bf16[8,4,192,512]{3,2,1,0:T(8,128)(2,1)} copy(bf16[8,4,192,512]{2,3,1,0:T(8,128)(2,1)} %fusion.21) | data formatting | bytes 12582912 | tf_op jit(solution)/shard_map/stack | solution.py:14
  207.6 146.0 %all_to_all.5 = bf16[8,4,192,512]{3,2,1,0:T(8,128)(2,1)S(1)} all-to-all(bf16[8,4,192,512]{3,2,1,0:T(8,128)(2,1)} %copy.29), channel_id=1, replica_groups=mesh['group'=2,'swap'=8,'image'=2] {'swap'}, dimensions={0} | all-to-all | bytes 12582912 | tf_op jit(solution)/shard_map/all_to_all | solution.py:14
  353.6 0.9 bitcast_reduce_fusion
  354.5 1.6 fusion.17
  356.2 4.4 fusion.15
  360.6 8.7 %copy.31 = bf16[4,512,1536]{2,1,0:T(8,128)(2,1)} copy(bf16[4,512,1536]{1,2,0:T(8,128)(2,1)} %bitcast.95) | data formatting | bytes 12582912 | tf_op jit(solution)/shard_map/convert_element_type | solution.py:81
  369.4 0.0 all-gather.3.cloned.1.call-update
  369.4 0.0 all-gather.5.cloned.1.call-start
  369.5 0.1 copy.32
  369.6 0.7 mul.87
  370.3 1.6 fusion.20
  371.9 0.0 all-gather.5.cloned.1.call-update
  371.9 0.0 all-reduce.4.cloned.1.call-start
  372.0 21.3 %all-gather.3.cloned.1.call-done = bf16[4096,1536]{1,0:T(8,128)(2,1)} async-done(((bf16[2048,1536]{1,0:T(8,128)(2,1)}), bf16[4096,1536]{1,0:T(8,128)(2,1)}) %all-gather.3.cloned.1.call-update) | async-done | bytes 12582928 | tf_op jit(solution)/shard_map/all_gather | solution.py:83
  393.3 8.3 %convolution_convert_fusion = bf16[4096,32]{0,1:T(8,128)(2,1)S(1)} fusion(bf16[4096,1536]{1,0:T(8,128)(2,1)} %all-gather.3.cloned.1.call-done, bf16[1536,32]{0,1:T(8,128)(2,1)S(1)} %copy-done.3), kind=kOutput, calls=%fused_computation.26 | convolution fusion | flops 402784256 | bytes 12943360 | tf_op jit(solution)/shard_map/dot_general | solution.py:89
  401.6 20.1 %fusion.29 = f32[4096,3072]{1,0:T(8,128)} fusion(bf16[4096,32]{0,1:T(8,128)(2,1)S(1)} %convolution_convert_fusion, bf16[32,3072]{1,0:T(8,128)(2,1)S(1)} %copy-done), kind=kOutput, calls=%fused_computation.50 | convolution fusion | flops 805306368 | bytes 50790400 | tf_op jit(solution)/shard_map/dot_general | solution.py:90
  421.7 112.2 %all-gather.5.cloned.1.call-done = bf16[1536,3072]{1,0:T(8,128)(2,1)} async-done(((bf16[192,3072]{1,0:T(8,128)(2,1)}), bf16[1536,3072]{1,0:T(8,128)(2,1)}) %all-gather.5.cloned.1.call-update) | async-done | bytes 9437200 | tf_op jit(solution)/shard_map/all_gather | solution.py:86
  533.9 64.7 %fusion.5 = bf16[4096,3072]{1,0:T(8,128)(2,1)} fusion(bf16[4096,3072]{1,0:T(8,128)(2,1)} %bitcast.97, f32[4096,3072]{1,0:T(8,128)} %fusion.29, bf16[4096,1536]{1,0:T(8,128)(2,1)} %all-gather.3.cloned.1.call-done, bf16[1536,3072]{1,0:T(8,128)(2,1)} %all-gather.5.cloned.1.call-done), kind=kOutput, calls=%fused_computation.6 | convolution fusion | flops 38818283520 | bytes 122683392 | tf_op jit(solution)/shard_map/dot_general | solution.py:88
  598.6 13.0 %fusion.30 = f32[4096,32]{0,1:T(8,128)} fusion(bf16[4096,3072]{1,0:T(8,128)(2,1)} %fusion.5, bf16[32,3072]{1,0:T(8,128)(2,1)S(1)} %copy-done), kind=kOutput, calls=%fused_computation.51 | convolution fusion | flops 805306368 | bytes 25886720 | tf_op jit(solution)/shard_map/dot_general | solution.py:96
  611.7 0.0 all-reduce.4.cloned.1.call-update
  611.7 0.0 all-reduce.6.cloned.1.call-start
  611.7 11.7 %convolution_multiply_fusion = f32[32,3072]{1,0:T(8,128)} fusion(bf16[4096,32]{0,1:T(8,128)(2,1)S(1)} %convolution_convert_fusion, bf16[4096,3072]{1,0:T(8,128)(2,1)} %fusion.5), kind=kOutput, calls=%fused_computation.27 | convolution fusion | flops 805404672 | bytes 25821184 | tf_op jit(solution)/shard_map/dot_general | solution.py:95
  623.4 5.2 all-reduce.4.cloned.1.call-done
  628.6 9.7 %convolution_multiply_fusion.1 = f32[1536,32]{0,1:T(8,128)} fusion(bf16[4096,1536]{1,0:T(8,128)(2,1)} %all-gather.3.cloned.1.call-done, f32[4096,32]{0,1:T(8,128)} %all-reduce.4.cloned.1.call-done), kind=kOutput, calls=%fused_computation.30 | convolution fusion | flops 2415968256 | bytes 13303808 | tf_op jit(solution)/shard_map/dot_general | solution.py:100
  638.4 74.7 %all-reduce.6.cloned.1.call-done = (f32[1536,32]{0,1:T(8,128)}, f32[32,3072]{1,0:T(8,128)}) async-done(((f32[1536,32]{0,1:T(8,128)}, f32[32,3072]{1,0:T(8,128)}), (f32[1536,32]{0,1:T(8,128)}, f32[32,3072]{1,0:T(8,128)})) %all-reduce.6.cloned.1.call-update) | async-done | bytes 589840 | tf_op jit(solution)/shard_map/psum | solution.py:107
  713.1 1.6 copy.55
  714.7 1.8 copy.56
  (21 shorter events, 0.1 us)
Async XLA Ops:
  7.2 394.4 %copy-start = (bf16[32,3072]{1,0:T(8,128)(2,1)S(1)}, bf16[32,3072]{1,0:T(8,128)(2,1)}, u32[]{:S(2)}) copy-start(bf16[32,3072]{1,0:T(8,128)(2,1)} %param.18) | copy-start | bytes 589828
  7.2 386.1 %all-gather.3.cloned.1.call-start = ((), (), s32[]{:S(2)}) async-start(), calls=%async_computation.1 | async-start | bytes 18874368 | tf_op jit(solution)/shard_map/all_gather | solution.py:83
  40.2 5.3 copy-start.1
  45.5 4.2 copy-start.8
  167.5 17.9 %copy-start.7 = (f32[192]{0:T(256)S(1)}, f32[192]{0:T(256)}, u32[]{:S(2)}) copy-start(f32[192]{0:T(256)} %param.12) | copy-start | bytes 2308
  207.6 148.6 %copy-start.5 = (f32[1536]{0:T(1024)S(1)}, f32[1536]{0:T(1024)}, u32[]{:S(2)}) copy-start(f32[1536]{0:T(1024)} %param.14) | copy-start | bytes 18436
  207.6 148.6 %copy-start.6 = (f32[1536]{0:T(1024)S(1)}, f32[1536]{0:T(1024)}, u32[]{:S(2)}) copy-start(f32[1536]{0:T(1024)} %param.13) | copy-start | bytes 18436
  360.6 8.8 %copy-start.4 = (s32[192,24]{0,1:T(8,128)S(1)}, s32[192,24]{0,1:T(8,128)}, u32[]{:S(2)}) copy-start(s32[192,24]{0,1:T(8,128)} %param.16) | copy-start | bytes 55300
  360.6 9.7 %copy-start.2 = (bf16[192,3072]{1,0:T(8,128)(2,1)S(1)}, bf16[192,3072]{1,0:T(8,128)(2,1)}, u32[]{:S(2)}) copy-start(bf16[192,3072]{1,0:T(8,128)(2,1)} %param.15) | copy-start | bytes 3538948
  360.6 32.7 %copy-start.3 = (bf16[1536,32]{0,1:T(8,128)(2,1)S(1)}, bf16[1536,32]{0,1:T(8,128)(2,1)}, u32[]{:S(2)}) copy-start(bf16[1536,32]{0,1:T(8,128)(2,1)} %param.17) | copy-start | bytes 294916
  369.4 164.5 %all-gather.5.cloned.1.call-start = ((), (), s32[]{:S(2)}) async-start(), calls=%async_computation.2 | async-start | bytes 10616832 | tf_op jit(solution)/shard_map/all_gather | solution.py:86
  371.9 256.7 %all-reduce.4.cloned.1.call-start = ((), (), s32[]{:S(2)}) async-start(), calls=%async_computation.3 | async-start | bytes 1048576 | tf_op jit(solution)/shard_map/psum | solution.py:99
  611.7 101.4 %all-reduce.6.cloned.1.call-start = ((), (), s32[]{:S(2)}) async-start(), calls=%async_computation.4 | async-start | bytes 1179648 | tf_op jit(solution)/shard_map/psum | solution.py:107
Sparse Core Ops, SparseCore 0:
  369.5 23.7 all-gather.2
  395.5 138.3 all-gather.4
  611.8 16.7 all-reduce.3
  638.5 74.4 all-reduce.5
